TPU v7x, 32 devices: a whole 2x2x4 slice. The times are simulated.
32 devices in a mesh: dp: 2 (over core), expert: 16 (over z, y, x).
Axes of the slice: x: 2, y: 2, z: 4, core: 2. Of those that a mesh axis runs over, the one named last changes fastest.
Arguments:
- tokens: bfloat16 [4096, 2048], P(('dp', 'expert')), may hold values from -6 to 6
- grad_out: bfloat16 [4096, 2048], P(('dp', 'expert')), may hold values from -6 to 6
- expert_ids: int32 [4096, 4], P(('dp', 'expert')), may hold values from 0 to 15, all different within a row; in each aligned block of 128 rows (0 to 127, 128 to 255, ...) at most 40 rows name the same one
- gate_values: bfloat16 [4096, 4], P(('dp', 'expert')), may hold values from 0.019897461 to 0.796875
- weight_in: bfloat16 [16, 2, 1408, 2048], P('expert', None, 'dp'), may hold values from -0.125 to 0.125
- weight_down: bfloat16 [16, 1408, 2048], P('expert', 'dp'), may hold values from -0.15625 to 0.15625
Outputs:
- grad_tokens: bfloat16 [4096, 2048], P(('dp', 'expert'))
- grad_gates: bfloat16 [4096, 4], P(('dp', 'expert'))
- grad_weight_in: bfloat16 [16, 2, 1408, 2048], P('expert', None, 'dp')
- grad_weight_down: bfloat16 [16, 1408, 2048], P('expert', 'dp')
Inputs may be any that keep to these rules, and one draw needn't show every extreme that they name: `expert_ids`: each row names 4 different experts. Within each aligned block of 128 rows (the rows of one device) no expert is named by more than 40 rows, and in some block some expert is named by exactly 40 rows.
All inputs are finite; a program needn't handle non-finite values.
Results may differ from a plain program's by a relative error of at most 0.008.
Values may be sent and summed in bfloat16 or wider, within the bound.
A program may use at most 128 MiB of HBM per device.

v0:
```python
import jax
import jax.numpy as jnp
from jax import lax
from jax.sharding import PartitionSpec as P


def expert_grads(inputs_rows, dy_rows, gate_rows, proj_in, proj_down):
    hidden = proj_in.shape[1]
    stacked = proj_in.reshape(2 * hidden, proj_in.shape[2])
    projected = lax.dot_general(
        inputs_rows, stacked, (((1,), (1,)), ((), ())), preferred_element_type=jnp.float32
    )
    gate_part = projected[:, :hidden]
    up_part = projected[:, hidden:]
    sigmoid_gate = jax.nn.sigmoid(gate_part)
    silu_gate = gate_part * sigmoid_gate
    hidden_act = (silu_gate * up_part).astype(jnp.bfloat16)
    upstream = lax.dot_general(
        dy_rows, proj_down, (((1,), (1,)), ((), ())), preferred_element_type=jnp.float32
    )
    gate_grad = jnp.sum(upstream * hidden_act.astype(jnp.float32), axis=1)
    gate_scale = gate_rows.astype(jnp.float32)[:, None]
    scaled_dy = (gate_scale * dy_rows.astype(jnp.float32)).astype(jnp.bfloat16)
    grad_down = lax.dot_general(
        hidden_act, scaled_dy, (((0,), (0,)), ((), ())), preferred_element_type=jnp.float32
    )
    hidden_grad = gate_scale * upstream
    grad_gate_part = (
        hidden_grad * up_part * sigmoid_gate * (1.0 + gate_part * (1.0 - sigmoid_gate))
    ).astype(jnp.bfloat16)
    grad_up_part = (hidden_grad * silu_gate).astype(jnp.bfloat16)
    joined = jnp.concatenate([grad_gate_part, grad_up_part], axis=1)
    row_grads = jnp.dot(joined, stacked, preferred_element_type=jnp.float32)
    grad_in = lax.dot_general(
        joined, inputs_rows, (((0,), (0,)), ((), ())), preferred_element_type=jnp.float32
    )
    return (row_grads, gate_grad, grad_in.reshape(2, hidden, proj_in.shape[2]), grad_down)


def slot_places(expert_ids, experts, capacity):
    flat_ids = expert_ids.reshape(-1)
    onehot = (flat_ids[:, None] == jnp.arange(experts, dtype=jnp.int32)[None, :]).astype(jnp.int32)
    running = jnp.cumsum(onehot, axis=0) - 1
    position = jnp.sum(onehot * running, axis=1)
    return flat_ids * capacity + position


def body(tokens, grad_out, expert_ids, gate_values, weight_in, weight_down):
    experts = lax.axis_size("expert")
    tok_rows = tokens.shape[0]
    feature_count = tokens.shape[1]
    top_count = expert_ids.shape[1]
    capacity = tok_rows * top_count * 5 // (4 * experts)
    slot_count = experts * capacity
    slot_index = slot_places(expert_ids, experts, capacity)
    pair_count = tok_rows * top_count
    owner_pair = (
        jnp.full((slot_count,), pair_count, jnp.int32)
        .at[slot_index]
        .set(jnp.arange(pair_count, dtype=jnp.int32))
    )
    token_of = owner_pair // top_count
    pad_row = jnp.zeros((1, feature_count), jnp.bfloat16)
    send_inputs = jnp.concatenate([tokens, pad_row], axis=0)[token_of].reshape(
        experts, capacity, feature_count
    )
    send_dy = jnp.concatenate([grad_out, pad_row], axis=0)[token_of].reshape(
        experts, capacity, feature_count
    )
    send_gate = jnp.concatenate([gate_values.reshape(-1), jnp.zeros((1,), jnp.bfloat16)])[
        owner_pair
    ].reshape(experts, capacity)
    recv_inputs, recv_dy, recv_gate = (
        lax.all_to_all(send_inputs, "expert", split_axis=0, concat_axis=0, tiled=True),
        lax.all_to_all(send_dy, "expert", split_axis=0, concat_axis=0, tiled=True),
        lax.all_to_all(send_gate, "expert", split_axis=0, concat_axis=0, tiled=True),
    )
    full_in, full_down = (
        lax.all_gather(weight_in, "dp", axis=2, tiled=True),
        lax.all_gather(weight_down, "dp", axis=1, tiled=True),
    )
    row_grads, gate_grad, grad_in, grad_down = expert_grads(
        recv_inputs.reshape(slot_count, feature_count),
        recv_dy.reshape(slot_count, feature_count),
        recv_gate.reshape(slot_count),
        full_in[0],
        full_down[0],
    )
    grad_in, grad_down = (
        lax.psum_scatter(grad_in, "dp", scatter_dimension=1, tiled=True),
        lax.psum_scatter(grad_down, "dp", scatter_dimension=0, tiled=True),
    )
    back_rows, back_gate = (
        lax.all_to_all(
            row_grads.astype(jnp.bfloat16).reshape(experts, capacity, feature_count),
            "expert",
            split_axis=0,
            concat_axis=0,
            tiled=True,
        ),
        lax.all_to_all(
            gate_grad.astype(jnp.bfloat16).reshape(experts, capacity),
            "expert",
            split_axis=0,
            concat_axis=0,
            tiled=True,
        ),
    )
    picked = back_rows.reshape(slot_count, feature_count)[slot_index].reshape(
        tok_rows, top_count, feature_count
    )
    grad_tokens = jnp.sum(picked, axis=1, dtype=jnp.float32).astype(jnp.bfloat16)
    grad_gates = back_gate.reshape(slot_count)[slot_index].reshape(tok_rows, top_count)
    return (
        grad_tokens,
        grad_gates,
        grad_in.astype(jnp.bfloat16)[None],
        grad_down.astype(jnp.bfloat16)[None],
    )


def solution(mesh):
    placed = (
        P(("dp", "expert"), None),
        P(("dp", "expert"), None),
        P(("dp", "expert"), None),
        P(("dp", "expert"), None),
        P("expert", None, "dp", None),
        P("expert", "dp", None),
    )
    return jax.shard_map(
        body,
        mesh=mesh,
        in_specs=placed,
        out_specs=(
            P(("dp", "expert"), None),
            P(("dp", "expert"), None),
            P("expert", None, "dp", None),
            P("expert", "dp", None),
        ),
        check_vma=False,
    )
```

profile of v0, /device:TPU:12, one launch (start us, length us, event | category | flops | bytes accessed | tf_op | source)
XLA Modules:
  0.0 318.7 jit_solution(16413516991251456437)
XLA Ops:
  7.2 0.0 copy-start.2
  7.2 0.0 copy-start.3
  7.2 0.0 copy-start.1
  7.2 0.0 all-gather.5.cloned.1.call-start
  7.2 0.7 all-gather.5.cloned.1.call-update
  7.9 0.0 copy-done.2
  7.9 0.1 copy.20
  8.1 0.1 eq.29
  8.2 0.1 eq.25
  8.3 0.0 copy-done.3
  8.3 0.1 copy.18
  8.4 0.1 reshape.117
  8.5 0.1 copy.19
  8.7 0.1 mul.61
  8.8 1.2 reduce-window.6
  9.9 0.2 slice_reduce_fusion
  10.2 0.1 fusion.7
  10.3 2.4 scatter_custom_fusion
  12.8 4.3 %gather_fusion = bf16[640]{0:T(1024)(128)(2,1)S(1)} fusion(bf16[513]{0:T(1024)(128)(2,1)S(1)} %pad_maximum_fusion.2, s32[1024]{0:T(1024)S(1)} %get-tuple-element.21), kind=kCustom, calls=%fused_computation | custom fusion | bytes 5120 | tf_op jit(solution)/shard_map/gather | solution.py:70
  17.1 0.7 all_to_all.25
  17.8 7.2 %all-to-all-start = ((bf16[16,1,40]{2,1,0:T(2,128)(2,1)}), bf16[16,1,40]{2,1,0:T(2,128)(2,1)S(1)}, u32[]{:S(2)}, u32[]{:S(2)}) async-start(bf16[16,1,40]{2,1,0:T(2,128)(2,1)} %all_to_all.25), calls=%async_computation | async-start | bytes 16384 | tf_op jit(solution)/shard_map/all_to_all | solution.py:76
  25.0 0.0 copy-done.1
  25.1 4.1 %gather_fusion.2 = bf16[640,2048]{1,0:T(8,128)(2,1)} fusion(bf16[129,2048]{1,0:T(8,128)(2,1)S(1)} %concatenate.14, s32[1024]{0:T(1024)S(1)} %get-tuple-element.20), kind=kCustom, calls=%fused_computation.2 | custom fusion | bytes 5245440 | tf_op jit(solution)/shard_map/gather | solution.py:64
  29.1 0.8 all-to-all-done
  29.9 6.1 %all-to-all-start.2 = ((bf16[16,40,2048]{2,1,0:T(8,128)(2,1)}), bf16[16,40,2048]{2,1,0:T(8,128)(2,1)S(1)}, u32[]{:S(2)}, u32[]{:S(2)}) async-start(bf16[16,40,2048]{2,1,0:T(8,128)(2,1)} %bitcast.6), calls=%async_computation.2 | async-start | bytes 5242880 | tf_op jit(solution)/shard_map/all_to_all | solution.py:74
  36.0 0.0 all-gather.3.cloned.1.call-start
  36.1 0.7 all-gather.3.cloned.1.call-update
  36.8 1.1 concatenate.13
  37.9 4.1 %gather_fusion.1 = bf16[640,2048]{1,0:T(8,128)(2,1)} fusion(bf16[129,2048]{1,0:T(8,128)(2,1)S(1)} %concatenate.13, s32[1024]{0:T(1024)S(1)} %get-tuple-element.20), kind=kCustom, calls=%fused_computation.1 | custom fusion | bytes 5245440 | tf_op jit(solution)/shard_map/gather | solution.py:67
  41.9 53.0 %all-to-all-done.2 = bf16[16,40,2048]{2,1,0:T(8,128)(2,1)S(1)} async-done(((bf16[16,40,2048]{2,1,0:T(8,128)(2,1)}), bf16[16,40,2048]{2,1,0:T(8,128)(2,1)S(1)}, u32[]{:S(2)}, u32[]{:S(2)}) %all-to-all-start.2) | async-done | bytes 2621472 | tf_op jit(solution)/shard_map/all_to_all | solution.py:74
  94.9 4.8 %all-to-all-start.1 = ((bf16[16,40,2048]{2,1,0:T(8,128)(2,1)}), bf16[16,40,2048]{2,1,0:T(8,128)(2,1)}, u32[]{:S(2)}, u32[]{:S(2)}) async-start(bf16[16,40,2048]{2,1,0:T(8,128)(2,1)} %bitcast.3), calls=%async_computation.1 | async-start | bytes 5242880 | tf_op jit(solution)/shard_map/all_to_all | solution.py:75
  99.7 0.2 reduce-scatter.5.cloned.1.call-start
  100.0 0.1 reshape.128
  100.0 0.0 all-gather.5.cloned.1.call-done
  100.1 13.1 %fusion.14 = f32[640,2816]{1,0:T(8,128)} fusion(bf16[640,2048]{1,0:T(8,128)(2,1)S(1)} %bitcast.48, bf16[2816,2048]{1,0:T(8,128)(2,1)} %bitcast.54), kind=kOutput, calls=%fused_computation.49 | convolution fusion | flops 7381975040 | bytes 21364736 | tf_op jit(solution)/shard_map/dot_general | solution.py:10
  113.1 45.3 %all-to-all-done.1 = bf16[16,40,2048]{2,1,0:T(8,128)(2,1)} async-done(((bf16[16,40,2048]{2,1,0:T(8,128)(2,1)}), bf16[16,40,2048]{2,1,0:T(8,128)(2,1)}, u32[]{:S(2)}, u32[]{:S(2)}) %all-to-all-start.1) | async-done | bytes 2621472 | tf_op jit(solution)/shard_map/all_to_all | solution.py:75
  158.4 0.0 all-gather.3.cloned.1.call-done
  158.4 12.4 %multiply_reduce_fusion = (bf16[640]{0:T(1024)(128)(2,1)S(1)}, bf16[640,1408]{1,0:T(8,128)(2,1)S(1)}, bf16[640,1408]{1,0:T(8,128)(2,1)}, bf16[640,1408]{1,0:T(8,128)(2,1)}) fusion(f32[640,2816]{1,0:T(8,128)} %fusion.14, f32[640]{0:T(1024)S(1)} %reshape.128, bf16[640,2048]{1,0:T(8,128)(2,1)} %bitcast.4, bf16[1,1408,2048]{2,1,0:T(8,128)(2,1)} %all-gather.3.cloned.1.call-done), kind=kOutput, calls=%fused_computation.11 | convolution fusion | flops 3708108288 | bytes 21008128 | tf_op jit(solution)/shard_map/dot_general | solution.py:18
  170.8 9.5 %fusion.3 = f32[1408,2048]{1,0:T(8,128)} fusion(bf16[640,1408]{1,0:T(8,128)(2,1)S(1)} %get-tuple-element.13, bf16[640,2048]{1,0:T(8,128)(2,1)} %bitcast.4, f32[640]{0:T(1024)S(1)} %reshape.128), kind=kOutput, calls=%fused_computation.19 | convolution fusion | flops 3694919680 | bytes 15960576 | tf_op jit(solution)/shard_map/dot_general | solution.py:24
  180.4 0.0 reduce-scatter.5.cloned.1.call-update
  180.4 0.3 reduce-scatter.3.cloned.1.call-start
  180.7 4.1 %fusion.5 = bf16[2816,640]{0,1:T(8,128)(2,1)} fusion(bf16[640,1408]{1,0:T(8,128)(2,1)} %get-tuple-element.16, bf16[640,1408]{1,0:T(8,128)(2,1)} %get-tuple-element.17), kind=kLoop, calls=%fused_computation.21 | loop fusion | flops 7208960 | bytes 7208960 | tf_op jit(solution)/shard_map/dot_general | solution.py:34
  184.8 6.3 %copy.27 = bf16[2816,640]{1,0:T(8,128)(2,1)} copy(bf16[2816,640]{0,1:T(8,128)(2,1)} %fusion.5) | data formatting | bytes 7208960 | tf_op jit(solution)/shard_map/dot_general | solution.py:34
  191.0 15.1 %fusion.15 = f32[2,1408,2048]{2,1,0:T(8,128)} fusion(bf16[2,1408,640]{2,1,0:T(8,128)(2,1)} %bitcast.47, bf16[640,2048,1]{1,0,2:T(8,128)(2,1)S(1)} %bitcast.49), kind=kOutput, calls=%fused_computation.50 | convolution fusion | flops 7381975040 | bytes 29294592 | tf_op jit(solution)/shard_map/dot_general | solution.py:34
  206.2 0.0 copy-start
  206.2 0.0 reduce-scatter.3.cloned.1.call-update
  206.2 0.7 convert_element_type.73
  206.9 5.3 %all-to-all-start.4 = ((bf16[16,1,40]{2,1,0:T(2,128)(2,1)}), bf16[16,1,40]{2,1,0:T(2,128)(2,1)S(1)}, u32[]{:S(2)}, u32[]{:S(2)}) async-start(bf16[16,1,40]{2,1,0:T(2,128)(2,1)} %convert_element_type.73), calls=%async_computation.4 | async-start | bytes 16384 | tf_op jit(solution)/shard_map/all_to_all | solution.py:101
  212.2 0.0 copy-done
  212.2 13.0 %convolution_convert_fusion = bf16[640,2048]{1,0:T(8,128)(2,1)} fusion(bf16[2816,2048]{1,0:T(8,128)(2,1)} %bitcast.55, bf16[640,1408]{1,0:T(8,128)(2,1)S(1)} %copy-done, bf16[640,1408]{1,0:T(8,128)(2,1)} %get-tuple-element.17), kind=kOutput, calls=%fused_computation.17 | convolution fusion | flops 7390494720 | bytes 17760256 | tf_op jit(solution)/shard_map/dot_general | solution.py:33
  225.2 0.0 all-to-all-done.4
  225.2 6.9 %all-to-all-start.3 = ((bf16[16,40,2048]{2,1,0:T(8,128)(2,1)}), bf16[16,40,2048]{2,1,0:T(8,128)(2,1)S(1)}, u32[]{:S(2)}, u32[]{:S(2)}) async-start(bf16[16,40,2048]{2,1,0:T(8,128)(2,1)} %bitcast.50), calls=%async_computation.3 | async-start | bytes 5242880 | tf_op jit(solution)/shard_map/all_to_all | solution.py:94
  232.1 0.1 reshape.126
  232.2 3.5 %gather_fusion.4 = bf16[512]{0:T(512)(128)(2,1)S(1)} fusion(bf16[640]{0:T(1024)(128)(2,1)S(1)} %reshape.126, s32[1024]{0:T(1024)S(1)} %pad_clamp_fusion), kind=kCustom, calls=%fused_computation.4 | custom fusion | bytes 4096 | tf_op jit(solution)/shard_map/gather | solution.py:113
  235.7 0.1 reshape.127
  235.9 0.7 copy.26
  236.5 53.4 %all-to-all-done.3 = bf16[16,40,2048]{2,1,0:T(8,128)(2,1)S(1)} async-done(((bf16[16,40,2048]{2,1,0:T(8,128)(2,1)}), bf16[16,40,2048]{2,1,0:T(8,128)(2,1)S(1)}, u32[]{:S(2)}, u32[]{:S(2)}) %all-to-all-start.3) | async-done | bytes 2621472 | tf_op jit(solution)/shard_map/all_to_all | solution.py:94
  290.0 3.3 %gather_fusion.3 = bf16[512,2048]{1,0:T(8,128)(2,1)} fusion(bf16[640,2048]{1,0:T(8,128)(2,1)S(1)} %bitcast.46, s32[1024]{0:T(1024)S(1)} %pad_clamp_fusion), kind=kCustom, calls=%fused_computation.3 | custom fusion | bytes 4196352 | tf_op jit(solution)/shard_map/gather | solution.py:109
  293.2 2.7 reshape.125
  296.0 3.9 %reduce_sum.34 = bf16[128,2048]{1,0:T(8,128)(2,1)} reduce(bf16[128,4,2048]{2,1,0:T(4,128)(2,1)S(1)} %reshape.125, bf16[]{:T(256)} %constant.37.clone.1), dimensions={1}, to_apply=%region_4.5 | reduce | flops 786432 | bytes 2621442 | tf_op jit(solution)/shard_map/reduce_sum | solution.py:112
  299.8 0.0 reduce-scatter.5.cloned.1.call-done
  299.8 4.7 %convert_bitcast_fusion.1 = bf16[1,704,2048]{2,1,0:T(8,128)(2,1)} fusion(f32[704,2048]{1,0:T(8,128)} %reduce-scatter.5.cloned.1.call-done), kind=kLoop, calls=%fused_computation.18 | loop fusion | flops 1441792 | bytes 8650752 | tf_op jit(solution)/shard_map/broadcast_in_dim | solution.py:118
  304.5 0.0 reduce-scatter.3.cloned.1.call-done
  304.5 7.7 %convert_bitcast_fusion = bf16[1,2,704,2048]{3,2,1,0:T(8,128)(2,1)} fusion(f32[2,704,2048]{2,1,0:T(8,128)} %reduce-scatter.3.cloned.1.call-done), kind=kLoop, calls=%fused_computation.8 | loop fusion | flops 2883584 | bytes 17301504 | tf_op jit(solution)/shard_map/broadcast_in_dim | solution.py:117
  (13 shorter events, 0.2 us)
Async XLA Ops:
  7.2 0.8 copy-start.2
  7.2 1.1 copy-start.3
  7.2 17.8 %copy-start.1 = (bf16[128,2048]{1,0:T(8,128)(2,1)S(1)}, bf16[128,2048]{1,0:T(8,128)(2,1)}, u32[]{:S(2)}) copy-start(bf16[128,2048]{1,0:T(8,128)(2,1)} %param.6) | copy-start | bytes 1572868
  7.2 92.9 %all-gather.5.cloned.1.call-start = ((), (), s32[]{:S(2)}) async-start(), calls=%async_computation.8 | async-start | bytes 17301504 | tf_op jit(solution)/shard_map/all_gather | solution.py:79
  17.8 12.1 %all-to-all-start = ((bf16[16,1,40]{2,1,0:T(2,128)(2,1)}), bf16[16,1,40]{2,1,0:T(2,128)(2,1)S(1)}, u32[]{:S(2)}, u32[]{:S(2)}) async-start(bf16[16,1,40]{2,1,0:T(2,128)(2,1)} %all_to_all.25), calls=%async_computation | async-start | bytes 16384 | tf_op jit(solution)/shard_map/all_to_all | solution.py:76
  29.9 65.0 %all-to-all-start.2 = ((bf16[16,40,2048]{2,1,0:T(8,128)(2,1)}), bf16[16,40,2048]{2,1,0:T(8,128)(2,1)S(1)}, u32[]{:S(2)}, u32[]{:S(2)}) async-start(bf16[16,40,2048]{2,1,0:T(8,128)(2,1)} %bitcast.6), calls=%async_computation.2 | async-start | bytes 5242880 | tf_op jit(solution)/shard_map/all_to_all | solution.py:74
  36.0 122.4 %all-gather.3.cloned.1.call-start = ((), (), s32[]{:S(2)}) async-start(), calls=%async_computation.7 | async-start | bytes 8650752 | tf_op jit(solution)/shard_map/all_gather | solution.py:80
  94.9 63.5 %all-to-all-start.1 = ((bf16[16,40,2048]{2,1,0:T(8,128)(2,1)}), bf16[16,40,2048]{2,1,0:T(8,128)(2,1)}, u32[]{:S(2)}, u32[]{:S(2)}) async-start(bf16[16,40,2048]{2,1,0:T(8,128)(2,1)} %bitcast.3), calls=%async_computation.1 | async-start | bytes 5242880 | tf_op jit(solution)/shard_map/all_to_all | solution.py:75
  99.7 200.1 %reduce-scatter.5.cloned.1.call-start = ((), (), s32[]{:S(2)}) async-start(), calls=%async_computation.10 | async-start | bytes 17301504 | tf_op jit(solution)/shard_map/reduce_scatter | solution.py:91
  180.4 124.1 %reduce-scatter.3.cloned.1.call-start = ((), (), s32[]{:S(2)}) async-start(), calls=%async_computation.9 | async-start | bytes 34603008 | tf_op jit(solution)/shard_map/reduce_scatter | solution.py:90
  206.2 6.0 %copy-start = (bf16[640,1408]{1,0:T(8,128)(2,1)S(1)}, bf16[640,1408]{1,0:T(8,128)(2,1)}, u32[]{:S(2)}) copy-start(bf16[640,1408]{1,0:T(8,128)(2,1)} %get-tuple-element.16) | copy-start | bytes 5406724
  206.9 18.3 %all-to-all-start.4 = ((bf16[16,1,40]{2,1,0:T(2,128)(2,1)}), bf16[16,1,40]{2,1,0:T(2,128)(2,1)S(1)}, u32[]{:S(2)}, u32[]{:S(2)}) async-start(bf16[16,1,40]{2,1,0:T(2,128)(2,1)} %convert_element_type.73), calls=%async_computation.4 | async-start | bytes 16384 | tf_op jit(solution)/shard_map/all_to_all | solution.py:101
  225.2 64.8 %all-to-all-start.3 = ((bf16[16,40,2048]{2,1,0:T(8,128)(2,1)}), bf16[16,40,2048]{2,1,0:T(8,128)(2,1)S(1)}, u32[]{:S(2)}, u32[]{:S(2)}) async-start(bf16[16,40,2048]{2,1,0:T(8,128)(2,1)} %bitcast.50), calls=%async_computation.3 | async-start | bytes 5242880 | tf_op jit(solution)/shard_map/all_to_all | solution.py:94
Sparse Core Ops, SparseCore 0:
  9.6 24.4 all-gather.4
  38.4 17.1 all-gather.2
  180.5 19.2 reduce-scatter.4
  206.3 32.5 reduce-scatter.2
where the time goes:
time: 319 us
  waiting for transfers between devices  154 us (48%)
  matrix products  63.1 us (20%)
  local copies, waits for them, and re-layouts  35.2 us (11%)
  starting transfers between devices  30.8 us (10%)
  other arithmetic  21.7 us (7%)
  between operations  14 us (4%)
    all_to_all x1, waiting for transfers between devices, body(): lax.all_to_all(row_grads.astype(jnp.bfloat16).reshape(experts, capacity,...  53.4 us
    all_to_all x1, waiting for transfers between devices, body(): lax.all_to_all(send_inputs, 'expert', split_axis=0, concat_axis=0, tiled=...  53 us
    all_to_all x1, waiting for transfers between devices, body(): lax.all_to_all(send_dy, 'expert', split_axis=0, concat_axis=0, tiled=True)  45.3 us
    dot_general x1, matrix products, expert_grads(): lax.dot_general(joined, inputs_rows, (((0,), (0,)), ((), ())), preferred_...  15.1 us
    dot_general x1, matrix products, expert_grads(): lax.dot_general(inputs_rows, stacked, (((1,), (1,)), ((), ())), preferred...  13.1 us
    dot_general x1, matrix products, expert_grads(): row_grads = jnp.dot(joined, stacked, preferred_element_type=jnp.float32)  13 us
    dot_general x1, matrix products, expert_grads(): lax.dot_general(dy_rows, proj_down, (((1,), (1,)), ((), ())), preferred_e...  12.4 us
    dot_general x1, matrix products, expert_grads(): lax.dot_general(hidden_act, scaled_dy, (((0,), (0,)), ((), ())), preferre...  9.54 us
  transfers between devices with their start and end apart: 9, of which 4 were waited for; matrix products, arithmetic and copies ran while one was open for 28% of the time, Pallas kernels for 0%

commit v1 on v0

v1 whole, which is shorter than its diff:
```python
import jax
import jax.numpy as jnp
from jax import lax
from jax.sharding import Mesh, PartitionSpec as P

BF16 = jnp.bfloat16
F32 = jnp.float32
ALL = ("dp", "z", "p")
SWAP = [(0, 1), (1, 0)]
BACK_CHUNKS = 2


def places(member):
    rows = member.shape[-1]
    before = (
        jnp.arange(rows, dtype=jnp.int32)[:, None] < jnp.arange(rows, dtype=jnp.int32)[None, :]
    ).astype(BF16)
    return jnp.einsum("...u,ut->...t", member.astype(BF16), before, preferred_element_type=F32)


def chosen(member, place, capacity):
    slots = jnp.arange(capacity, dtype=jnp.int32).astype(F32)[:, None]
    return member[..., None, :] & (place[..., None, :] == slots)


def hop(value, step, right, nz):
    if right:
        pairs = [(i, i + 1) for i in range(nz - 1) if i <= step]
    else:
        pairs = [(i, i - 1) for i in range(1, nz) if i >= nz - 1 - step]
    return lax.ppermute(value, "z", pairs)


def spread(value, z, nz):
    lefts, rights = [value], [value]
    for k in range(1, nz):
        lefts.append(lax.ppermute(lefts[-1], "z", [(i, i + 1) for i in range(k - 1, nz - 1)]))
        rights.append(lax.ppermute(rights[-1], "z", [(i, i - 1) for i in range(1, nz - k + 1)]))
    blocks = [value] + [jnp.where(z >= m, lefts[m], rights[nz - m]) for m in range(1, nz)]
    return jnp.concatenate(blocks, axis=0), (lefts[-1], rights[-1])


def collect(part, nz):
    from_left = from_right = None
    for step in range(nz - 1):
        go_right, go_left = part[step + 1], part[nz - 1 - step]
        if step:
            go_right = (go_right.astype(F32) + from_left.astype(F32)).astype(BF16)
            go_left = (go_left.astype(F32) + from_right.astype(F32)).astype(BF16)
        from_left = hop(go_right, step, True, nz)
        from_right = hop(go_left, step, False, nz)
    return part[0].astype(F32) + from_left.astype(F32) + from_right.astype(F32)


def body(tokens, grad_out, expert_ids, gate_values, weight_in, weight_down):
    nz, npl = lax.axis_size("z"), lax.axis_size("p")
    z, p = lax.axis_index("z"), lax.axis_index("p")
    experts = nz * npl
    rows, width = tokens.shape
    top = expert_ids.shape[1]
    cap = rows * top * 5 // (4 * experts)
    half = experts * cap
    hidden = weight_down.shape[1]

    tagged = jnp.concatenate(
        [
            tokens,
            expert_ids.astype(BF16),
            gate_values,
            jnp.zeros((rows, 128 - 2 * top), BF16),
        ],
        axis=1,
    )
    tok_col, arrived = spread(tagged, z, nz)
    grad_out, _ = lax.optimization_barrier((grad_out, arrived))
    dy_col, _ = spread(grad_out, z, nz)

    ids_col = tok_col[:, width : width + top].astype(jnp.int32).reshape(nz, rows, top)
    plane = z * npl + jnp.arange(npl, dtype=jnp.int32)
    named = ids_col[None] == plane[:, None, None, None]
    member = jnp.any(named, axis=-1)
    sel = chosen(member, places(member), cap)
    same = jnp.arange(nz)[:, None] == jnp.arange(nz)[None, :]
    pick = (sel[:, :, :, None, :] & same[None, :, None, :, None]).astype(BF16)
    pick = pick.reshape(half, nz * rows)

    def route(col):
        send = jnp.dot(pick, col, preferred_element_type=F32).astype(BF16)
        return lax.all_to_all(
            send.reshape(npl, nz * cap, -1), "p", split_axis=0, concat_axis=0, tiled=True
        ).reshape(half, -1)

    own, dy_col = lax.optimization_barrier((route(tok_col), dy_col))
    far = lax.ppermute(own, "dp", SWAP)
    x = jnp.concatenate([own[:, :width], far[:, :width]], axis=0)
    tags = jnp.concatenate([own[:, width:], far[:, width:]], axis=0)

    mine = tags[:, :top].astype(jnp.int32) == z * npl + p
    g = jnp.sum(jnp.where(mine, tags[:, top : 2 * top].astype(F32), 0.0), axis=1)[:, None]

    w_gate, w_up, w_down = weight_in[0, 0], weight_in[0, 1], weight_down[0]
    w_both = weight_in.reshape(2 * hidden, width)
    across = (((1,), (1,)), ((), ()))
    a = lax.dot_general(x, w_gate, across, preferred_element_type=F32)
    b = lax.dot_general(x, w_up, across, preferred_element_type=F32)
    own_y, a, b = lax.optimization_barrier((route(dy_col), a, b))
    y = jnp.concatenate([own_y, lax.ppermute(own_y, "dp", SWAP)], axis=0)
    sig = jax.nn.sigmoid(a)
    silu = a * sig
    h = (silu * b).astype(BF16)
    u = lax.dot_general(y, w_down, across, preferred_element_type=F32)
    gate_grad = jnp.sum(u * h.astype(F32), axis=1)
    hg = g * u
    da = (hg * b * sig * (1.0 + a * (1.0 - sig))).astype(BF16)
    db = (hg * silu).astype(BF16)
    dab = jnp.concatenate([da, db], axis=1)
    s = (g * y.astype(F32)).astype(BF16)

    inner = (((0,), (0,)), ((), ()))

    high = gate_grad[half:].astype(BF16)
    low = (gate_grad[half:] - high.astype(F32)).astype(BF16)
    outs, weight_grads = [], []
    step = width // BACK_CHUNKS
    for c in range(BACK_CHUNKS):
        w_cols = w_both[:, c * step : (c + 1) * step]
        far_r = jnp.dot(dab[half:], w_cols, preferred_element_type=F32).astype(BF16)
        if c == 0:
            far_r = jnp.concatenate(
                [far_r, high[:, None], low[:, None], jnp.zeros((half, 126), BF16)], axis=1
            )
        came = lax.ppermute(far_r, "dp", SWAP)
        near_r = jnp.dot(dab[:half], w_cols, preferred_element_type=F32)
        r = (near_r + came[:, :step].astype(F32)).astype(BF16)
        if c == 0:
            pg = gate_grad[:half] + came[:, step].astype(F32) + came[:, step + 1].astype(F32)
            r = jnp.concatenate([r, pg.astype(BF16)[:, None], jnp.zeros((half, 127), BF16)], axis=1)
        if c == 0:
            r, lhs, rhs = lax.optimization_barrier((r, dab, x))
        else:
            r, lhs, rhs = lax.optimization_barrier((r, h, s))
        grad_w = lax.dot_general(lhs, rhs, inner, preferred_element_type=F32).astype(BF16)
        back = lax.all_to_all(
            r.reshape(npl, nz * cap, -1), "p", split_axis=0, concat_axis=0, tiled=True
        ).reshape(half, -1)
        back, grad_w = lax.optimization_barrier((back, grad_w))
        weight_grads.append(grad_w)
        part = lax.dot_general(
            pick, back[:, :step], (((0,), (0,)), ((), ())), preferred_element_type=F32
        ).astype(BF16)
        if c == 0:
            slot_pg = back[:, step].astype(F32).reshape(npl, nz, cap)
            row_pg = jnp.sum(jnp.where(sel, slot_pg[..., None], 0.0), axis=2)
            row_pg = jnp.sum(jnp.where(named, row_pg[..., None], 0.0), axis=0)
            row_pg = row_pg.reshape(nz * rows, top).astype(BF16)
            part = jnp.concatenate(
                [part, row_pg, jnp.zeros((nz * rows, 128 - top), BF16)], axis=1
            )
        outs.append(collect(part.reshape(nz, rows, -1), nz))
    grad_gates = outs[0][:, step : step + top].astype(BF16)
    outs[0] = outs[0][:, :step]
    grad_tokens = jnp.concatenate([o.astype(BF16) for o in outs], axis=1)

    gw_in, gw_down = weight_grads
    return grad_tokens, grad_gates, gw_in.reshape(weight_in.shape), gw_down[None]


def solution(mesh):
    nz = 4
    experts = mesh.shape["expert"]
    split = Mesh(
        mesh.devices.reshape(mesh.shape["dp"], nz, experts // nz), ALL
    )
    rows = P(ALL, None)
    w_in = P(("z", "p"), None, "dp", None)
    w_down = P(("z", "p"), "dp", None)
    return jax.shard_map(
        body,
        mesh=split,
        in_specs=(rows, rows, rows, rows, w_in, w_down),
        out_specs=(rows, rows, w_in, w_down),
        check_vma=False,
    )
```

time: 319 us -> 288 us (0.903)
  waiting for transfers between devices: 154 us -> 74.1 us
  starting transfers between devices: 30.8 us -> 78.4 us
  between operations: 14 us -> 1.44 us
  matrix products: 63.1 us -> 73.9 us
  other arithmetic: 21.7 us -> 31.4 us
  local copies, waits for them, and re-layouts: 35.2 us -> 26.4 us
    all_to_all x5 -> x4, waiting for transfers between devices: 153 us -> 27.8 us  [the longest x2 27.5 us: route(): lax.all_to_all(send.reshape(npl, nz * cap, -1), 'p', split_axis=0, concat...]
    ppermute x0 -> x28, starting transfers between devices: none -> 58.9 us  [the longest x12 27.3 us: hop(): return lax.ppermute(value, 'z', pairs)]
    ppermute x0 -> x28, waiting for transfers between devices: none -> 46.3 us  [the longest x6 18.6 us: spread(): lax.ppermute(lefts[-1], 'z', [(i, i + 1) for i in range(k - 1, nz - 1)])]
    gather x5 -> x0, local copies, waits for them, and re-layouts: 19.2 us -> none  [the longest x1 4.3 us: body(): jnp.concatenate([gate_values.reshape(-1), jnp.zeros((1,), jnp.bfloat16)])]
    convert_element_type x2 -> x12, other arithmetic: 0.03 us -> 13.9 us  [the longest x1 5.9 us: body(): s = (g * y.astype(F32)).astype(BF16)]
    broadcast_in_dim x2 -> x0, other arithmetic: 12.4 us -> none  [the longest x1 7.71 us: body(): grad_in.astype(jnp.bfloat16)[None]]
    dot_general x5 -> x14, matrix products: 63.1 us -> 73.9 us  [the longest x2 21 us: body(): lax.dot_general(lhs, rhs, inner, preferred_element_type=F32).astype(BF16)]
    all_to_all x5 -> x4, starting transfers between devices: 30.2 us -> 19.6 us  [the longest x2 10.1 us: route(): lax.all_to_all(send.reshape(npl, nz * cap, -1), 'p', split_axis=0, concat...]
  transfers between devices with their start and end apart: 9 -> 32, of which waited for: 4 -> 13; matrix products, arithmetic and copies ran while one was open for 28% -> 38% of each run, Pallas kernels for 0% -> 0%
where the time goes in v1:
time: 288 us; the launch traced here: 286 us
  starting transfers between devices  78.4 us (27%)
  waiting for transfers between devices  74.1 us (26%)
  matrix products  73.9 us (26%)
  other arithmetic  31.4 us (11%)
  local copies, waits for them, and re-layouts  26.4 us (9%)
    all_to_all x2, waiting for transfers between devices, route(): lax.all_to_all(send.reshape(npl, nz * cap, -1), 'p', split_axis=0, concat...  27.5 us
    ppermute x12, starting transfers between devices, hop(): return lax.ppermute(value, 'z', pairs)  27.3 us
    dot_general x2, matrix products, body(): lax.dot_general(lhs, rhs, inner, preferred_element_type=F32).astype(BF16)  21 us
    ppermute x6, waiting for transfers between devices, spread(): lax.ppermute(lefts[-1], 'z', [(i, i + 1) for i in range(k - 1, nz - 1)])  18.6 us
    ppermute x6, waiting for transfers between devices, spread(): lax.ppermute(rights[-1], 'z', [(i, i - 1) for i in range(1, nz - k + 1)])  18.1 us
    ppermute x6, starting transfers between devices, spread(): lax.ppermute(rights[-1], 'z', [(i, i - 1) for i in range(1, nz - k + 1)])  16.8 us
    ppermute x6, starting transfers between devices, spread(): lax.ppermute(lefts[-1], 'z', [(i, i + 1) for i in range(k - 1, nz - 1)])  14.2 us
    dot_general x2, matrix products, body(): near_r = jnp.dot(dab[:half], w_cols, preferred_element_type=F32)  11 us
  transfers between devices with their start and end apart: 32, of which 13 were waited for; matrix products, arithmetic and copies ran while one was open for 38% of the time, Pallas kernels for 0%

profile of v1, /device:TPU:12, one launch (start us, length us, event | category | flops | bytes accessed | tf_op | source)
XLA Modules:
  0.0 285.6 jit_solution(9133891994225016165)
XLA Ops:
  3.6 3.5 %collective-permute-start = (bf16[128,2176]{1,0:T(8,128)(2,1)S(1)}, bf16[128,2176]{1,0:T(8,128)(2,1)}, u32[]{:S(2)}, u32[]{:S(2)}) collective-permute-start(bf16[128,2176]{1,0:T(8,128)(2,1)S(1)} %concatenate.33), channel_id=1, source_target_pairs={{0,4},{4,8},{8,12},{1,5},{5,9},{9,13},{2,6},{6,10},{10,14},{3,7},{... | collective-permute-start | bytes 1671176 | tf_op jit(solution)/shard_map/ppermute | solution.py:37
  7.1 3.1 %collective-permute-start.1 = (bf16[128,2176]{1,0:T(8,128)(2,1)S(1)}, bf16[128,2176]{1,0:T(8,128)(2,1)}, u32[]{:S(2)}, u32[]{:S(2)}) collective-permute-start(bf16[128,2176]{1,0:T(8,128)(2,1)S(1)} %concatenate.33), channel_id=1, source_target_pairs={{4,0},{8,4},{12,8},{5,1},{9,5},{13,9},{6,2},{10,6},{14,10},{7,3},{... | collective-permute-start | bytes 1671176 | tf_op jit(solution)/shard_map/ppermute | solution.py:38
  10.3 9.7 %collective-permute-done = bf16[128,2176]{1,0:T(8,128)(2,1)} collective-permute-done((bf16[128,2176]{1,0:T(8,128)(2,1)S(1)}, bf16[128,2176]{1,0:T(8,128)(2,1)}, u32[]{:S(2)}, u32[]{:S(2)}) %collective-permute-start) | collective-permute-done | bytes 557088 | tf_op jit(solution)/shard_map/ppermute | solution.py:37
  20.0 4.3 %collective-permute-start.4 = (bf16[128,2176]{1,0:T(8,128)(2,1)}, bf16[128,2176]{1,0:T(8,128)(2,1)}, u32[]{:S(2)}, u32[]{:S(2)}) collective-permute-start(bf16[128,2176]{1,0:T(8,128)(2,1)} %collective-permute-done), channel_id=1, source_target_pairs={{4,8},{8,12},{5,9},{9,13},{6,10},{10,14},{7,11},{11,15},{20,24},{2... | collective-permute-start | bytes 1671176 | tf_op jit(solution)/shard_map/ppermute | solution.py:37
  24.3 2.0 collective-permute-start.2
  26.4 8.4 %collective-permute-done.4 = bf16[128,2176]{1,0:T(8,128)(2,1)} collective-permute-done((bf16[128,2176]{1,0:T(8,128)(2,1)}, bf16[128,2176]{1,0:T(8,128)(2,1)}, u32[]{:S(2)}, u32[]{:S(2)}) %collective-permute-start.4) | collective-permute-done | bytes 557088 | tf_op jit(solution)/shard_map/ppermute | solution.py:37
  35.5 4.2 %collective-permute-done.2 = bf16[128,2176]{1,0:T(8,128)(2,1)} collective-permute-done((bf16[128,2176]{1,0:T(8,128)(2,1)}, bf16[128,2176]{1,0:T(8,128)(2,1)}, u32[]{:S(2)}, u32[]{:S(2)}) %collective-permute-start.2) | collective-permute-done | bytes 557088 | tf_op jit(solution)/shard_map/ppermute | solution.py:38
  39.7 2.2 collective-permute-start.3
  43.1 9.0 %collective-permute-done.3 = bf16[128,2176]{1,0:T(8,128)(2,1)S(1)} collective-permute-done((bf16[128,2176]{1,0:T(8,128)(2,1)}, bf16[128,2176]{1,0:T(8,128)(2,1)S(1)}, u32[]{:S(2)}, u32[]{:S(2)}) %collective-permute-start.3) | collective-permute-done | bytes 557088 | tf_op jit(solution)/shard_map/ppermute | solution.py:38
  52.1 1.9 collective-permute-start.6
  54.1 4.7 %collective-permute-start.7 = (bf16[128,2048]{1,0:T(8,128)(2,1)}, bf16[128,2048]{1,0:T(8,128)(2,1)}, u32[]{:S(2)}, u32[]{:S(2)}) collective-permute-start(bf16[128,2048]{1,0:T(8,128)(2,1)} %param.7), channel_id=1, source_target_pairs={{4,0},{8,4},{12,8},{5,1},{9,5},{13,9},{6,2},{10,6},{14,10},{7,3},{... | collective-permute-start | bytes 1572872 | tf_op jit(solution)/shard_map/ppermute | solution.py:38
  59.9 1.3 broadcast_select_fusion.2
  65.2 3.0 %collective-permute-start.10 = (bf16[128,2048]{1,0:T(8,128)(2,1)}, bf16[128,2048]{1,0:T(8,128)(2,1)}, u32[]{:S(2)}, u32[]{:S(2)}) collective-permute-start(bf16[128,2048]{1,0:T(8,128)(2,1)} %collective-permute-done.6), channel_id=1, source_target_pairs={{4,8},{8,12},{5,9},{9,13},{6,10},{10,14},{7,11},{11,15},{20,24},{2... | collective-permute-start | bytes 1572872 | tf_op jit(solution)/shard_map/ppermute | solution.py:37
  68.2 3.4 %collective-permute-start.8 = (bf16[128,2048]{1,0:T(8,128)(2,1)}, bf16[128,2048]{1,0:T(8,128)(2,1)}, u32[]{:S(2)}, u32[]{:S(2)}) collective-permute-start(bf16[128,2048]{1,0:T(8,128)(2,1)} %collective-permute-done.7), channel_id=1, source_target_pairs={{4,0},{8,4},{5,1},{9,5},{6,2},{10,6},{7,3},{11,7},{20,16},{24,20},... | collective-permute-start | bytes 1572872 | tf_op jit(solution)/shard_map/ppermute | solution.py:38
  71.5 4.6 %convolution_convert_fusion.1 = bf16[640,2176]{1,0:T(8,128)(2,1)} fusion(bf16[128,2176]{1,0:T(8,128)(2,1)} %copy-done.9, bf16[128,2176]{1,0:T(8,128)(2,1)S(1)} %broadcast_select_fusion.1, bf16[128,2176]{1,0:T(8,128)(2,1)} %copy-done.10, bf16[128,2176]{1,0:T(8,128)(2,1)} %copy-done.11, pred[80,8,4,128]{3,2,1,0:T(4,128)(4,1)S(1)} %bitcast.52), kind=kOutput, calls=%fused_computation.3 | convolution fusion | flops 1436368896 | bytes 5341184 | tf_op jit(solution)/shard_map/dot_general | solution.py:88
  76.2 5.1 %all-to-all-start = ((bf16[4,160,2176]{2,1,0:T(8,128)(2,1)}), bf16[4,160,2176]{2,1,0:T(8,128)(2,1)}, u32[]{:S(2)}, u32[]{:S(2)}) async-start(bf16[4,160,2176]{2,1,0:T(8,128)(2,1)} %bitcast.47), calls=%async_computation | async-start | bytes 5570560 | tf_op jit(solution)/shard_map/all_to_all | solution.py:89
  82.1 1.3 collective-permute-start.9
  85.7 4.9 %collective-permute-done.9 = bf16[128,2048]{1,0:T(8,128)(2,1)S(1)} collective-permute-done((bf16[128,2048]{1,0:T(8,128)(2,1)}, bf16[128,2048]{1,0:T(8,128)(2,1)S(1)}, u32[]{:S(2)}, u32[]{:S(2)}) %collective-permute-start.9) | collective-permute-done | bytes 524320 | tf_op jit(solution)/shard_map/ppermute | solution.py:38
  91.6 1.6 pad_maximum_fusion.2
  93.2 15.8 %all-to-all-done = bf16[4,160,2176]{2,1,0:T(8,128)(2,1)} async-done(((bf16[4,160,2176]{2,1,0:T(8,128)(2,1)}), bf16[4,160,2176]{2,1,0:T(8,128)(2,1)}, u32[]{:S(2)}, u32[]{:S(2)}) %all-to-all-start) | async-done | bytes 2785312 | tf_op jit(solution)/shard_map/all_to_all | solution.py:89
  109.0 4.6 %convolution_convert_fusion.3 = bf16[640,2048]{1,0:T(8,128)(2,1)} fusion(bf16[512,2048]{1,0:T(8,128)(2,1)} %pad_maximum_fusion.2, pred[80,8,4,128]{3,2,1,0:T(4,128)(4,1)S(1)} %bitcast.53), kind=kOutput, calls=%fused_computation.16 | convolution fusion | flops 1343488000 | bytes 5046272 | tf_op jit(solution)/shard_map/dot_general | solution.py:88
  113.6 5.1 %all-to-all-start.1 = ((bf16[4,160,2048]{2,1,0:T(8,128)(2,1)}), bf16[4,160,2048]{2,1,0:T(8,128)(2,1)}, u32[]{:S(2)}, u32[]{:S(2)}) async-start(bf16[4,160,2048]{2,1,0:T(8,128)(2,1)} %bitcast.48), calls=%async_computation.1 | async-start | bytes 5242880 | tf_op jit(solution)/shard_map/all_to_all | solution.py:89
  118.7 1.9 slice.114
  120.6 2.9 %slice.142 = bf16[640,2048]{1,0:T(8,128)(2,1)S(1)} slice(bf16[640,2176]{1,0:T(8,128)(2,1)} %collective-permute-done.12), slice={[0:640], [0:2048]} | slice | bytes 5242880 | tf_op jit(solution)/shard_map/slice | solution.py:95
  123.6 8.6 %fusion.5 = f32[1280,704]{0,1:T(8,128)} fusion(bf16[1,2,704,2048]{3,2,1,0:T(8,128)(2,1)} %param.10, bf16[640,2048]{1,0:T(8,128)(2,1)S(1)} %slice.142, bf16[640,2048]{1,0:T(8,128)(2,1)S(1)} %slice.114), kind=kOutput, calls=%fused_computation.21 | convolution fusion | flops 3701473280 | bytes 11730944 | tf_op jit(solution)/shard_map/dot_general | solution.py:104
  132.2 5.8 %fusion.3 = f32[1280,704]{0,1:T(8,128)} fusion(bf16[1,2,704,2048]{3,2,1,0:T(8,128)(2,1)S(1)} %bitcast.59, bf16[640,2048]{1,0:T(8,128)(2,1)S(1)} %slice.142, bf16[640,2048]{1,0:T(8,128)(2,1)S(1)} %slice.114), kind=kOutput, calls=%fused_computation.19 | convolution fusion | flops 3701473280 | bytes 11730944 | tf_op jit(solution)/shard_map/dot_general | solution.py:105
  138.0 11.7 %all-to-all-done.1 = bf16[4,160,2048]{2,1,0:T(8,128)(2,1)} async-done(((bf16[4,160,2048]{2,1,0:T(8,128)(2,1)}), bf16[4,160,2048]{2,1,0:T(8,128)(2,1)}, u32[]{:S(2)}, u32[]{:S(2)}) %all-to-all-start.1) | async-done | bytes 2621472 | tf_op jit(solution)/shard_map/all_to_all | solution.py:89
  152.0 2.1 constant_dynamic-update-slice_fusion.1
  154.2 2.9 %pad_maximum_fusion = bf16[1280,2048]{1,0:T(8,128)(2,1)} fusion(bf16[640,2048]{1,0:T(8,128)(2,1)S(1)} %copy-done.6, bf16[640,2048]{1,0:T(8,128)(2,1)S(1)} %copy-done.4), kind=kLoop, calls=%fused_computation.2 | loop fusion | flops 10485760 | bytes 10485760 | tf_op jit(solution)/shard_map/concatenate | solution.py:95
  157.2 2.1 constant_dynamic-update-slice_fusion
  160.1 6.8 %multiply_reduce_fusion = (f32[1280]{0:T(1024)S(1)}, bf16[1280,704]{0,1:T(8,128)(2,1)}, bf16[1280,704]{0,1:T(8,128)(2,1)S(1)}, bf16[1280,704]{0,1:T(8,128)(2,1)S(1)}) fusion(f32[1280,704]{0,1:T(8,128)S(1)} %copy-done.22, f32[1280,704]{0,1:T(8,128)S(1)} %copy-done.21, f32[1280]{0:T(1024)S(1)} %select_reduce_fusion, ...), kind=kOutput, calls=%fused_computation.9 | convolution fusion | flops 3708107520 | bytes 20752384 | tf_op jit(solution)/shard_map/dot_general | solution.py:111
  166.9 3.3 %fusion.29 = bf16[640,1024]{1,0:T(8,128)(2,1)} fusion(bf16[1408,2048]{1,0:T(8,128)(2,1)S(1)} %bitcast.62, bf16[1280,704]{0,1:T(8,128)(2,1)S(1)} %get-tuple-element.58, bf16[1280,704]{0,1:T(8,128)(2,1)S(1)} %get-tuple-element.59), kind=kOutput, calls=%fused_computation.46 | convolution fusion | flops 1849753600 | bytes 7798784 | tf_op jit(solution)/shard_map/dot_general | solution.py:127
  170.2 2.2 fusion.26
  172.5 2.1 pad_maximum_fusion.1
  175.5 1.9 concatenate.40
  177.4 5.9 %multiply_convert_fusion = bf16[1280,2048]{1,0:T(8,128)(2,1)} fusion(bf16[1280,2048]{1,0:T(8,128)(2,1)} %copy-done.2, f32[1280]{0:T(1024)S(1)} %select_reduce_fusion), kind=kLoop, calls=%fused_computation | loop fusion | flops 7864320 | bytes 10490880 | tf_op jit(solution)/shard_map/convert_element_type | solution.py:117
  183.3 5.5 %add_convert_fusion = bf16[640,1024]{1,0:T(8,128)(2,1)} fusion(bf16[640,1024]{1,0:T(8,128)(2,1)} %collective-permute-done.21, bf16[1408,2048]{1,0:T(8,128)(2,1)} %bitcast.56, bf16[1280,704]{0,1:T(8,128)(2,1)S(1)} %copy-done.14, bf16[1280,704]{0,1:T(8,128)(2,1)S(1)} %copy-done.16), kind=kOutput, calls=%fused_computation.25 | convolution fusion | flops 1851064320 | bytes 9109504 | tf_op jit(solution)/shard_map/dot_general | solution.py:133
  188.9 4.8 %all-to-all-start.3 = ((bf16[4,160,1024]{2,1,0:T(8,128)(2,1)}), bf16[4,160,1024]{2,1,0:T(8,128)(2,1)}, u32[]{:S(2)}, u32[]{:S(2)}) async-start(bf16[4,160,1024]{2,1,0:T(8,128)(2,1)} %bitcast.49), calls=%async_computation.3 | async-start | bytes 2621440 | tf_op jit(solution)/shard_map/all_to_all | solution.py:143
  193.7 8.6 %convolution_convert_fusion.2 = bf16[704,2048]{1,0:T(8,128)(2,1)} fusion(bf16[1280,704]{0,1:T(8,128)(2,1)} %get-tuple-element.31, bf16[1280,2048]{1,0:T(8,128)(2,1)} %multiply_convert_fusion), kind=kOutput, calls=%fused_computation.15 | convolution fusion | flops 3692429312 | bytes 9928704 | tf_op jit(solution)/shard_map/dot_general | solution.py:142
  202.3 1.2 convert_reduce_fusion.2
  203.7 5.5 %add_convert_fusion.1 = bf16[640,1024]{1,0:T(8,128)(2,1)} fusion(bf16[640,1152]{1,0:T(8,128)(2,1)} %collective-permute-done.14, bf16[1408,2048]{1,0:T(8,128)(2,1)} %bitcast.57, bf16[1280,704]{0,1:T(8,128)(2,1)S(1)} %copy-done.14, bf16[1280,704]{0,1:T(8,128)(2,1)S(1)} %copy-done.17), kind=kOutput, calls=%fused_computation.26 | convolution fusion | flops 1851064320 | bytes 9109504 | tf_op jit(solution)/shard_map/dot_general | solution.py:133
  209.2 3.6 %concatenate.41 = bf16[640,1152]{1,0:T(8,128)(2,1)} concatenate(bf16[640,1024]{1,0:T(8,128)(2,1)} %add_convert_fusion.1, bf16[640,1]{1,0:T(8,128)(2,1)S(1)} %broadcast_in_dim.78, bf16[640,127]{1,0:T(8,128)(2,1)S(1)} %broadcast_in_dim.69), dimensions={1} | concatenate | bytes 2949120 | tf_op jit(solution)/shard_map/concatenate | solution.py:137
  212.9 4.6 %all-to-all-start.2 = ((bf16[4,160,1152]{2,1,0:T(8,128)(2,1)}), bf16[4,160,1152]{2,1,0:T(8,128)(2,1)}, u32[]{:S(2)}, u32[]{:S(2)}) async-start(bf16[4,160,1152]{2,1,0:T(8,128)(2,1)} %bitcast.10), calls=%async_computation.2 | async-start | bytes 2949120 | tf_op jit(solution)/shard_map/all_to_all | solution.py:143
  217.5 12.4 %convolution_convert_fusion = bf16[1408,2048]{1,0:T(8,128)(2,1)} fusion(bf16[1280,1408]{0,1:T(8,128)(2,1)} %pad_maximum_fusion.1, bf16[1280,2048]{1,0:T(8,128)(2,1)} %pad_maximum_fusion), kind=kOutput, calls=%fused_computation.1 | convolution fusion | flops 7384858624 | bytes 14614528 | tf_op jit(solution)/shard_map/dot_general | solution.py:142
  229.9 2.3 convolution_convert_fusion.4
  233.1 1.3 collective-permute-start.22
  234.4 1.4 collective-permute-start.25
  236.2 3.3 %convolution_convert_fusion.5 = bf16[512,1024]{1,0:T(8,128)(2,1)} fusion(bf16[640,1152]{1,0:T(8,128)(2,1)} %bitcast.11, pred[80,8,4,128]{3,2,1,0:T(4,128)(4,1)S(1)} %bitcast.55), kind=kOutput, calls=%fused_computation.48 | convolution fusion | flops 671612928 | bytes 2686976 | tf_op jit(solution)/shard_map/dot_general | solution.py:148
  241.2 2.4 concatenate.42
  243.7 1.3 collective-permute-start.15
  246.8 3.6 %collective-permute-start.23 = (bf16[128,1024]{1,0:T(8,128)(2,1)S(1)}, bf16[128,1024]{1,0:T(8,128)(2,1)S(1)}, u32[]{:S(2)}, u32[]{:S(2)}) collective-permute-start(bf16[128,1024]{1,0:T(8,128)(2,1)S(1)} %get-tuple-element.68), channel_id=1, source_target_pairs={{0,4},{4,8},{1,5},{5,9},{2,6},{6,10},{3,7},{7,11},{16,20},{20,24},... | collective-permute-start | bytes 786440 | tf_op jit(solution)/shard_map/ppermute | solution.py:31
  250.4 1.3 collective-permute-start.26
  251.7 3.8 %collective-permute-done.15 = bf16[128,1152]{1,0:T(8,128)(2,1)S(1)} collective-permute-done((bf16[128,1152]{1,0:T(8,128)(2,1)S(1)}, bf16[128,1152]{1,0:T(8,128)(2,1)S(1)}, u32[]{:S(2)}, u32[]{:S(2)}) %collective-permute-start.15) | collective-permute-done | bytes 294944 | tf_op jit(solution)/shard_map/ppermute | solution.py:31
  255.6 4.2 %collective-permute-start.16 = (bf16[128,1152]{1,0:T(8,128)(2,1)S(1)}, bf16[128,1152]{1,0:T(8,128)(2,1)S(1)}, u32[]{:S(2)}, u32[]{:S(2)}) collective-permute-start(bf16[128,1152]{1,0:T(8,128)(2,1)S(1)} %get-tuple-element.62), channel_id=1, source_target_pairs={{0,4},{4,8},{1,5},{5,9},{2,6},{6,10},{3,7},{7,11},{16,20},{20,24},... | collective-permute-start | bytes 884744 | tf_op jit(solution)/shard_map/ppermute | solution.py:31
  259.8 1.3 collective-permute-start.19
  261.2 1.4 add_convert_fusion.7
  262.5 1.9 collective-permute-start.27
  264.5 4.6 %collective-permute-start.24 = (bf16[128,1024]{1,0:T(8,128)(2,1)S(1)}, bf16[128,1024]{1,0:T(8,128)(2,1)S(1)}, u32[]{:S(2)}, u32[]{:S(2)}) collective-permute-start(bf16[128,1024]{1,0:T(8,128)(2,1)S(1)} %get-tuple-element.66), channel_id=1, source_target_pairs={{0,4},{4,8},{8,12},{1,5},{5,9},{9,13},{2,6},{6,10},{10,14},{3,7},{... | collective-permute-start | bytes 786440 | tf_op jit(solution)/shard_map/ppermute | solution.py:31
  269.0 2.2 collective-permute-done.19
  271.3 1.2 add_convert_fusion.4
  272.4 1.9 collective-permute-start.20
  274.4 3.9 %collective-permute-start.17 = (bf16[128,1152]{1,0:T(8,128)(2,1)S(1)}, bf16[128,1152]{1,0:T(8,128)(2,1)S(1)}, u32[]{:S(2)}, u32[]{:S(2)}) collective-permute-start(bf16[128,1152]{1,0:T(8,128)(2,1)S(1)} %get-tuple-element.60), channel_id=1, source_target_pairs={{0,4},{4,8},{8,12},{1,5},{5,9},{9,13},{2,6},{6,10},{10,14},{3,7},{... | collective-permute-start | bytes 884744 | tf_op jit(solution)/shard_map/ppermute | solution.py:31
  279.4 1.7 collective-permute-done.20
  281.1 1.9 collective-permute-done.17
  (130 shorter events, 26.8 us)
Async XLA Ops:
  0.6 158.6 %copy-start = (bf16[1,704,2048]{2,1,0:T(8,128)(2,1)S(1)}, bf16[1,704,2048]{2,1,0:T(8,128)(2,1)}, u32[]{:S(2)}) copy-start(bf16[1,704,2048]{2,1,0:T(8,128)(2,1)} %param.11) | copy-start | bytes 8650756
  3.6 36.1 %copy-start.11 = (bf16[128,2176]{1,0:T(8,128)(2,1)}, bf16[128,2176]{1,0:T(8,128)(2,1)S(1)}, u32[]{:S(2)}) copy-start(bf16[128,2176]{1,0:T(8,128)(2,1)S(1)} %concatenate.33) | copy-start | bytes 1671172
  3.6 16.4 %collective-permute-start = (bf16[128,2176]{1,0:T(8,128)(2,1)S(1)}, bf16[128,2176]{1,0:T(8,128)(2,1)}, u32[]{:S(2)}, u32[]{:S(2)}) collective-permute-start(bf16[128,2176]{1,0:T(8,128)(2,1)S(1)} %concatenate.33), channel_id=1, source_target_pairs={{0,4},{4,8},{8,12},{1,5},{5,9},{9,13},{2,6},{6,10},{10,14},{3,7},{... | collective-permute-start | bytes 1671176 | tf_op jit(solution)/shard_map/ppermute | solution.py:37
  7.1 17.2 %collective-permute-start.1 = (bf16[128,2176]{1,0:T(8,128)(2,1)S(1)}, bf16[128,2176]{1,0:T(8,128)(2,1)}, u32[]{:S(2)}, u32[]{:S(2)}) collective-permute-start(bf16[128,2176]{1,0:T(8,128)(2,1)S(1)} %concatenate.33), channel_id=1, source_target_pairs={{4,0},{8,4},{12,8},{5,1},{9,5},{13,9},{6,2},{10,6},{14,10},{7,3},{... | collective-permute-start | bytes 1671176 | tf_op jit(solution)/shard_map/ppermute | solution.py:38
  20.0 14.8 %collective-permute-start.4 = (bf16[128,2176]{1,0:T(8,128)(2,1)}, bf16[128,2176]{1,0:T(8,128)(2,1)}, u32[]{:S(2)}, u32[]{:S(2)}) collective-permute-start(bf16[128,2176]{1,0:T(8,128)(2,1)} %collective-permute-done), channel_id=1, source_target_pairs={{4,8},{8,12},{5,9},{9,13},{6,10},{10,14},{7,11},{11,15},{20,24},{2... | collective-permute-start | bytes 1671176 | tf_op jit(solution)/shard_map/ppermute | solution.py:37
  24.3 15.4 %collective-permute-start.2 = (bf16[128,2176]{1,0:T(8,128)(2,1)}, bf16[128,2176]{1,0:T(8,128)(2,1)}, u32[]{:S(2)}, u32[]{:S(2)}) collective-permute-start(bf16[128,2176]{1,0:T(8,128)(2,1)} %collective-permute-done.1), channel_id=1, source_target_pairs={{4,0},{8,4},{5,1},{9,5},{6,2},{10,6},{7,3},{11,7},{20,16},{24,20},... | collective-permute-start | bytes 1671176 | tf_op jit(solution)/shard_map/ppermute | solution.py:38
  34.8 8.4 %collective-permute-start.5 = (bf16[128,2176]{1,0:T(8,128)(2,1)}, bf16[128,2176]{1,0:T(8,128)(2,1)S(1)}, u32[]{:S(2)}, u32[]{:S(2)}) collective-permute-start(bf16[128,2176]{1,0:T(8,128)(2,1)} %collective-permute-done.4), channel_id=1, source_target_pairs={{8,12},{9,13},{10,14},{11,15},{24,28},{25,29},{26,30},{27,31}} | collective-permute-start | bytes 1671176 | tf_op jit(solution)/shard_map/ppermute | solution.py:37
  39.7 12.4 %collective-permute-start.3 = (bf16[128,2176]{1,0:T(8,128)(2,1)}, bf16[128,2176]{1,0:T(8,128)(2,1)S(1)}, u32[]{:S(2)}, u32[]{:S(2)}) collective-permute-start(bf16[128,2176]{1,0:T(8,128)(2,1)} %collective-permute-done.2), channel_id=1, source_target_pairs={{4,0},{5,1},{6,2},{7,3},{20,16},{21,17},{22,18},{23,19}} | collective-permute-start | bytes 1671176 | tf_op jit(solution)/shard_map/ppermute | solution.py:38
  41.9 19.3 %copy-start.12 = (bf16[128,2176]{1,0:T(8,128)(2,1)S(1)}, bf16[128,2176]{1,0:T(8,128)(2,1)}, u32[]{:S(2)}) copy-start(bf16[128,2176]{1,0:T(8,128)(2,1)} %copy-done.11) | copy-start | bytes 1671172
  52.1 13.0 %collective-permute-start.6 = (bf16[128,2048]{1,0:T(8,128)(2,1)}, bf16[128,2048]{1,0:T(8,128)(2,1)}, u32[]{:S(2)}, u32[]{:S(2)}) collective-permute-start(bf16[128,2048]{1,0:T(8,128)(2,1)} %param.7), channel_id=1, source_target_pairs={{0,4},{4,8},{8,12},{1,5},{5,9},{9,13},{2,6},{6,10},{10,14},{3,7},{... | collective-permute-start | bytes 1572872 | tf_op jit(solution)/shard_map/ppermute | solution.py:37
  54.1 14.1 %collective-permute-start.7 = (bf16[128,2048]{1,0:T(8,128)(2,1)}, bf16[128,2048]{1,0:T(8,128)(2,1)}, u32[]{:S(2)}, u32[]{:S(2)}) collective-permute-start(bf16[128,2048]{1,0:T(8,128)(2,1)} %param.7), channel_id=1, source_target_pairs={{4,0},{8,4},{12,8},{5,1},{9,5},{13,9},{6,2},{10,6},{14,10},{7,3},{... | collective-permute-start | bytes 1572872 | tf_op jit(solution)/shard_map/ppermute | solution.py:38
  59.9 1.3 copy-start.9
  61.3 0.8 copy-start.10
  64.7 11.5 %copy-start.19 = (pred[4,4,40,4,128]{4,3,2,1,0:T(4,128)(4,1)}, pred[4,4,40,4,128]{4,3,2,1,0:T(4,128)(4,1)S(1)}, u32[]{:S(2)}) copy-start(pred[4,4,40,4,128]{4,3,2,1,0:T(4,128)(4,1)S(1)} %broadcast_and_fusion) | copy-start | bytes 983044
  65.2 16.1 %collective-permute-start.10 = (bf16[128,2048]{1,0:T(8,128)(2,1)}, bf16[128,2048]{1,0:T(8,128)(2,1)}, u32[]{:S(2)}, u32[]{:S(2)}) collective-permute-start(bf16[128,2048]{1,0:T(8,128)(2,1)} %collective-permute-done.6), channel_id=1, source_target_pairs={{4,8},{8,12},{5,9},{9,13},{6,10},{10,14},{7,11},{11,15},{20,24},{2... | collective-permute-start | bytes 1572872 | tf_op jit(solution)/shard_map/ppermute | solution.py:37
  68.2 13.9 %collective-permute-start.8 = (bf16[128,2048]{1,0:T(8,128)(2,1)}, bf16[128,2048]{1,0:T(8,128)(2,1)}, u32[]{:S(2)}, u32[]{:S(2)}) collective-permute-start(bf16[128,2048]{1,0:T(8,128)(2,1)} %collective-permute-done.7), channel_id=1, source_target_pairs={{4,0},{8,4},{5,1},{9,5},{6,2},{10,6},{7,3},{11,7},{20,16},{24,20},... | collective-permute-start | bytes 1572872 | tf_op jit(solution)/shard_map/ppermute | solution.py:38
  76.2 32.8 %all-to-all-start = ((bf16[4,160,2176]{2,1,0:T(8,128)(2,1)}), bf16[4,160,2176]{2,1,0:T(8,128)(2,1)}, u32[]{:S(2)}, u32[]{:S(2)}) async-start(bf16[4,160,2176]{2,1,0:T(8,128)(2,1)} %bitcast.47), calls=%async_computation | async-start | bytes 5570560 | tf_op jit(solution)/shard_map/all_to_all | solution.py:89
  81.2 10.4 %copy-start.18 = (bf16[128,2048]{1,0:T(8,128)(2,1)S(1)}, bf16[128,2048]{1,0:T(8,128)(2,1)}, u32[]{:S(2)}) copy-start(bf16[128,2048]{1,0:T(8,128)(2,1)} %param.7) | copy-start | bytes 1572868
  81.2 3.3 %collective-permute-start.11 = (bf16[128,2048]{1,0:T(8,128)(2,1)}, bf16[128,2048]{1,0:T(8,128)(2,1)S(1)}, u32[]{:S(2)}, u32[]{:S(2)}) collective-permute-start(bf16[128,2048]{1,0:T(8,128)(2,1)} %collective-permute-done.10), channel_id=1, source_target_pairs={{8,12},{9,13},{10,14},{11,15},{24,28},{25,29},{26,30},{27,31}} | collective-permute-start | bytes 1572872 | tf_op jit(solution)/shard_map/ppermute | solution.py:37
  82.1 8.5 %collective-permute-start.9 = (bf16[128,2048]{1,0:T(8,128)(2,1)}, bf16[128,2048]{1,0:T(8,128)(2,1)S(1)}, u32[]{:S(2)}, u32[]{:S(2)}) collective-permute-start(bf16[128,2048]{1,0:T(8,128)(2,1)} %collective-permute-done.8), channel_id=1, source_target_pairs={{4,0},{5,1},{6,2},{7,3},{20,16},{21,17},{22,18},{23,19}} | collective-permute-start | bytes 1572872 | tf_op jit(solution)/shard_map/ppermute | solution.py:38
  85.6 23.3 %copy-start.20 = (pred[4,4,40,4,128]{4,3,2,1,0:T(4,128)(4,1)S(1)}, pred[4,4,40,4,128]{4,3,2,1,0:T(4,128)(4,1)}, u32[]{:S(2)}) copy-start(pred[4,4,40,4,128]{4,3,2,1,0:T(4,128)(4,1)} %copy-done.19) | copy-start | bytes 983044
  109.0 11.6 %collective-permute-start.12 = (bf16[640,2176]{1,0:T(8,128)(2,1)}, bf16[640,2176]{1,0:T(8,128)(2,1)}, u32[]{:S(2)}, u32[]{:S(2)}) collective-permute-start(bf16[640,2176]{1,0:T(8,128)(2,1)} %bitcast.3), channel_id=1, source_target_pairs={{0,16},{16,0},{1,17},{17,1},{2,18},{18,2},{3,19},{19,3},{4,20},{20... | collective-permute-start | bytes 8355848 | tf_op jit(solution)/shard_map/ppermute | solution.py:94
  113.6 36.1 %all-to-all-start.1 = ((bf16[4,160,2048]{2,1,0:T(8,128)(2,1)}), bf16[4,160,2048]{2,1,0:T(8,128)(2,1)}, u32[]{:S(2)}, u32[]{:S(2)}) async-start(bf16[4,160,2048]{2,1,0:T(8,128)(2,1)} %bitcast.48), calls=%async_computation.1 | async-start | bytes 5242880 | tf_op jit(solution)/shard_map/all_to_all | solution.py:89
  120.6 11.6 %copy-start.3 = (bf16[640,2048]{1,0:T(8,128)(2,1)}, bf16[640,2048]{1,0:T(8,128)(2,1)S(1)}, u32[]{:S(2)}) copy-start(bf16[640,2048]{1,0:T(8,128)(2,1)S(1)} %slice.114) | copy-start | bytes 7864324
  120.6 11.6 %slice-start = ((s8[5767168]{0:T(1024)(128)(4,1)}), s8[4194304]{0:T(1024)(128)(4,1)S(1)}, s32[]{:S(2)}) async-start(s8[5767168]{0:T(1024)(128)(4,1)} %bitcast.58), calls=%async_computation.4 | async-start | bytes 8388608
  123.5 8.7 %copy-start.5 = (bf16[640,2048]{1,0:T(8,128)(2,1)}, bf16[640,2048]{1,0:T(8,128)(2,1)S(1)}, u32[]{:S(2)}) copy-start(bf16[640,2048]{1,0:T(8,128)(2,1)S(1)} %slice.142) | copy-start | bytes 7864324
  123.5 8.7 %slice-start.1 = ((s8[5767168]{0:T(1024)(128)(4,1)}), s8[1572864]{0:T(1024)(128)(4,1)S(1)}, s32[]{:S(2)}) async-start(s8[5767168]{0:T(1024)(128)(4,1)} %bitcast.58), calls=%async_computation.5 | async-start | bytes 3145728
  149.7 7.5 %collective-permute-start.13 = (bf16[640,2048]{1,0:T(8,128)(2,1)}, bf16[640,2048]{1,0:T(8,128)(2,1)}, u32[]{:S(2)}, u32[]{:S(2)}) collective-permute-start(bf16[640,2048]{1,0:T(8,128)(2,1)} %bitcast.5), channel_id=1, source_target_pairs={{0,16},{16,0},{1,17},{17,1},{2,18},{18,2},{3,19},{19,3},{4,20},{20... | collective-permute-start | bytes 7864328 | tf_op jit(solution)/shard_map/ppermute | solution.py:107
  150.6 3.6 %copy-start.4 = (bf16[640,2048]{1,0:T(8,128)(2,1)S(1)}, bf16[640,2048]{1,0:T(8,128)(2,1)}, u32[]{:S(2)}) copy-start(bf16[640,2048]{1,0:T(8,128)(2,1)} %copy-done.3) | copy-start | bytes 7864324
  150.6 3.6 %copy-start.6 = (bf16[640,2048]{1,0:T(8,128)(2,1)S(1)}, bf16[640,2048]{1,0:T(8,128)(2,1)}, u32[]{:S(2)}) copy-start(bf16[640,2048]{1,0:T(8,128)(2,1)} %copy-done.5) | copy-start | bytes 7864324
  154.2 5.0 %copy-start.22 = (f32[1280,704]{0,1:T(8,128)S(1)}, f32[1280,704]{0,1:T(8,128)}, u32[]{:S(2)}) copy-start(f32[1280,704]{0,1:T(8,128)} %fusion.3) | copy-start | bytes 10813444
  157.1 3.0 %copy-start.21 = (f32[1280,704]{0,1:T(8,128)S(1)}, f32[1280,704]{0,1:T(8,128)}, u32[]{:S(2)}) copy-start(f32[1280,704]{0,1:T(8,128)} %fusion.5) | copy-start | bytes 10813444
  157.2 9.8 %slice-start.2 = ((s8[5767168]{0:T(1024)(128)(4,1)}), s8[4194304]{0:T(1024)(128)(4,1)S(1)}, s32[]{:S(2)}) async-start(s8[5767168]{0:T(1024)(128)(4,1)} %bitcast.60), calls=%async_computation.6 | async-start | bytes 8388608
  160.1 6.8 %copy-start.2 = (bf16[1280,2048]{1,0:T(8,128)(2,1)}, bf16[1280,2048]{1,0:T(8,128)(2,1)S(1)}, u32[]{:S(2)}) copy-start(bf16[1280,2048]{1,0:T(8,128)(2,1)S(1)} %constant_dynamic-update-slice_fusion) | copy-start | bytes 15728644
  160.1 6.8 %slice-start.3 = ((s8[5767168]{0:T(1024)(128)(4,1)}), s8[1572864]{0:T(1024)(128)(4,1)S(1)}, s32[]{:S(2)}) async-start(s8[5767168]{0:T(1024)(128)(4,1)} %bitcast.60), calls=%async_computation.7 | async-start | bytes 3145728
  166.9 5.6 %copy-start.13 = (bf16[1280,704]{0,1:T(8,128)(2,1)}, bf16[1280,704]{0,1:T(8,128)(2,1)S(1)}, u32[]{:S(2)}) copy-start(bf16[1280,704]{0,1:T(8,128)(2,1)S(1)} %get-tuple-element.58) | copy-start | bytes 5406724
  166.9 5.6 %copy-start.15 = (bf16[1280,704]{0,1:T(8,128)(2,1)}, bf16[1280,704]{0,1:T(8,128)(2,1)S(1)}, u32[]{:S(2)}) copy-start(bf16[1280,704]{0,1:T(8,128)(2,1)S(1)} %get-tuple-element.59) | copy-start | bytes 5406724
  174.6 8.7 %collective-permute-start.21 = (bf16[640,1024]{1,0:T(8,128)(2,1)}, bf16[640,1024]{1,0:T(8,128)(2,1)}, u32[]{:S(2)}, u32[]{:S(2)}) collective-permute-start(bf16[640,1024]{1,0:T(8,128)(2,1)} %fusion.29), channel_id=1, source_target_pairs={{0,16},{16,0},{1,17},{17,1},{2,18},{18,2},{3,19},{19,3},{4,20},{20... | collective-permute-start | bytes 3932168 | tf_op jit(solution)/shard_map/ppermute | solution.py:132
  177.4 5.9 %copy-start.14 = (bf16[1280,704]{0,1:T(8,128)(2,1)S(1)}, bf16[1280,704]{0,1:T(8,128)(2,1)}, u32[]{:S(2)}) copy-start(bf16[1280,704]{0,1:T(8,128)(2,1)} %copy-done.13) | copy-start | bytes 5406724
  177.4 5.9 %copy-start.16 = (bf16[1280,704]{0,1:T(8,128)(2,1)S(1)}, bf16[1280,704]{0,1:T(8,128)(2,1)}, u32[]{:S(2)}) copy-start(bf16[1280,704]{0,1:T(8,128)(2,1)} %copy-done.15) | copy-start | bytes 5406724
  177.4 24.9 %collective-permute-start.14 = (bf16[640,1152]{1,0:T(8,128)(2,1)}, bf16[640,1152]{1,0:T(8,128)(2,1)}, u32[]{:S(2)}, u32[]{:S(2)}) collective-permute-start(bf16[640,1152]{1,0:T(8,128)(2,1)} %concatenate.40), channel_id=1, source_target_pairs={{0,16},{16,0},{1,17},{17,1},{2,18},{18,2},{3,19},{19,3},{4,20},{20... | collective-permute-start | bytes 4423688 | tf_op jit(solution)/shard_map/ppermute | solution.py:132
  188.9 24.0 %all-to-all-start.3 = ((bf16[4,160,1024]{2,1,0:T(8,128)(2,1)}), bf16[4,160,1024]{2,1,0:T(8,128)(2,1)}, u32[]{:S(2)}, u32[]{:S(2)}) async-start(bf16[4,160,1024]{2,1,0:T(8,128)(2,1)} %bitcast.49), calls=%async_computation.3 | async-start | bytes 2621440 | tf_op jit(solution)/shard_map/all_to_all | solution.py:143
  193.7 10.0 %copy-start.17 = (bf16[1280,704]{0,1:T(8,128)(2,1)S(1)}, bf16[1280,704]{0,1:T(8,128)(2,1)}, u32[]{:S(2)}) copy-start(bf16[1280,704]{0,1:T(8,128)(2,1)} %copy-done.15) | copy-start | bytes 5406724
  212.9 23.3 %all-to-all-start.2 = ((bf16[4,160,1152]{2,1,0:T(8,128)(2,1)}), bf16[4,160,1152]{2,1,0:T(8,128)(2,1)}, u32[]{:S(2)}, u32[]{:S(2)}) async-start(bf16[4,160,1152]{2,1,0:T(8,128)(2,1)} %bitcast.10), calls=%async_computation.2 | async-start | bytes 2949120 | tf_op jit(solution)/shard_map/all_to_all | solution.py:143
  232.2 13.4 %copy-start.8 = (bf16[512,1024]{1,0:T(8,128)(2,1)}, bf16[512,1024]{1,0:T(8,128)(2,1)S(1)}, u32[]{:S(2)}) copy-start(bf16[512,1024]{1,0:T(8,128)(2,1)S(1)} %convolution_convert_fusion.4) | copy-start | bytes 3145732
  233.1 12.5 %collective-permute-start.22 = (bf16[128,1024]{1,0:T(8,128)(2,1)}, bf16[128,1024]{1,0:T(8,128)(2,1)S(1)}, u32[]{:S(2)}, u32[]{:S(2)}) collective-permute-start(bf16[128,1024]{1,0:T(8,128)(2,1)} %get-tuple-element.70), channel_id=1, source_target_pairs={{0,4},{1,5},{2,6},{3,7},{16,20},{17,21},{18,22},{19,23}} | collective-permute-start | bytes 786440 | tf_op jit(solution)/shard_map/ppermute | solution.py:31
  234.4 11.2 %collective-permute-start.25 = (bf16[128,1024]{1,0:T(8,128)(2,1)}, bf16[128,1024]{1,0:T(8,128)(2,1)}, u32[]{:S(2)}, u32[]{:S(2)}) collective-permute-start(bf16[128,1024]{1,0:T(8,128)(2,1)} %get-tuple-element.71), channel_id=1, source_target_pairs={{12,8},{13,9},{14,10},{15,11},{28,24},{29,25},{30,26},{31,27}} | collective-permute-start | bytes 786440 | tf_op jit(solution)/shard_map/ppermute | solution.py:31
  243.6 11.8 %copy-start.7 = (bf16[512,1152]{1,0:T(8,128)(2,1)}, bf16[512,1152]{1,0:T(8,128)(2,1)S(1)}, u32[]{:S(2)}) copy-start(bf16[512,1152]{1,0:T(8,128)(2,1)S(1)} %concatenate.42) | copy-start | bytes 3538948
  243.7 11.8 %collective-permute-start.15 = (bf16[128,1152]{1,0:T(8,128)(2,1)S(1)}, bf16[128,1152]{1,0:T(8,128)(2,1)S(1)}, u32[]{:S(2)}, u32[]{:S(2)}) collective-permute-start(bf16[128,1152]{1,0:T(8,128)(2,1)S(1)} %get-tuple-element.64), channel_id=1, source_target_pairs={{0,4},{1,5},{2,6},{3,7},{16,20},{17,21},{18,22},{19,23}} | collective-permute-start | bytes 884744 | tf_op jit(solution)/shard_map/ppermute | solution.py:31
  245.0 10.5 %collective-permute-start.18 = (bf16[128,1152]{1,0:T(8,128)(2,1)S(1)}, bf16[128,1152]{1,0:T(8,128)(2,1)S(1)}, u32[]{:S(2)}, u32[]{:S(2)}) collective-permute-start(bf16[128,1152]{1,0:T(8,128)(2,1)S(1)} %get-tuple-element.65), channel_id=1, source_target_pairs={{12,8},{13,9},{14,10},{15,11},{28,24},{29,25},{30,26},{31,27}} | collective-permute-start | bytes 884744 | tf_op jit(solution)/shard_map/ppermute | solution.py:31
  246.8 14.3 %collective-permute-start.23 = (bf16[128,1024]{1,0:T(8,128)(2,1)S(1)}, bf16[128,1024]{1,0:T(8,128)(2,1)S(1)}, u32[]{:S(2)}, u32[]{:S(2)}) collective-permute-start(bf16[128,1024]{1,0:T(8,128)(2,1)S(1)} %get-tuple-element.68), channel_id=1, source_target_pairs={{0,4},{4,8},{1,5},{5,9},{2,6},{6,10},{3,7},{7,11},{16,20},{20,24},... | collective-permute-start | bytes 786440 | tf_op jit(solution)/shard_map/ppermute | solution.py:31
  250.4 10.8 %collective-permute-start.26 = (bf16[128,1024]{1,0:T(8,128)(2,1)S(1)}, bf16[128,1024]{1,0:T(8,128)(2,1)S(1)}, u32[]{:S(2)}, u32[]{:S(2)}) collective-permute-start(bf16[128,1024]{1,0:T(8,128)(2,1)S(1)} %get-tuple-element.69), channel_id=1, source_target_pairs={{8,4},{12,8},{9,5},{13,9},{10,6},{14,10},{11,7},{15,11},{24,20},{2... | collective-permute-start | bytes 786440 | tf_op jit(solution)/shard_map/ppermute | solution.py:31
  255.6 13.5 %collective-permute-start.16 = (bf16[128,1152]{1,0:T(8,128)(2,1)S(1)}, bf16[128,1152]{1,0:T(8,128)(2,1)S(1)}, u32[]{:S(2)}, u32[]{:S(2)}) collective-permute-start(bf16[128,1152]{1,0:T(8,128)(2,1)S(1)} %get-tuple-element.62), channel_id=1, source_target_pairs={{0,4},{4,8},{1,5},{5,9},{2,6},{6,10},{3,7},{7,11},{16,20},{20,24},... | collective-permute-start | bytes 884744 | tf_op jit(solution)/shard_map/ppermute | solution.py:31
  259.8 11.4 %collective-permute-start.19 = (bf16[128,1152]{1,0:T(8,128)(2,1)S(1)}, bf16[128,1152]{1,0:T(8,128)(2,1)S(1)}, u32[]{:S(2)}, u32[]{:S(2)}) collective-permute-start(bf16[128,1152]{1,0:T(8,128)(2,1)S(1)} %get-tuple-element.63), channel_id=1, source_target_pairs={{8,4},{12,8},{9,5},{13,9},{10,6},{14,10},{11,7},{15,11},{24,20},{2... | collective-permute-start | bytes 884744 | tf_op jit(solution)/shard_map/ppermute | solution.py:31
  261.1 24.5 %copy-start.1 = (bf16[1,704,2048]{2,1,0:T(8,128)(2,1)S(1)}, bf16[1,704,2048]{2,1,0:T(8,128)(2,1)}, u32[]{:S(2)}) copy-start(bf16[1,704,2048]{2,1,0:T(8,128)(2,1)} %param.11) | copy-start | bytes 8650756
  262.5 15.8 %collective-permute-start.27 = (bf16[128,1024]{1,0:T(8,128)(2,1)S(1)}, bf16[128,1024]{1,0:T(8,128)(2,1)S(1)}, u32[]{:S(2)}, u32[]{:S(2)}) collective-permute-start(bf16[128,1024]{1,0:T(8,128)(2,1)S(1)} %get-tuple-element.67), channel_id=1, source_target_pairs={{4,0},{8,4},{12,8},{5,1},{9,5},{13,9},{6,2},{10,6},{14,10},{7,3},{... | collective-permute-start | bytes 786440 | tf_op jit(solution)/shard_map/ppermute | solution.py:31
  264.5 13.8 %collective-permute-start.24 = (bf16[128,1024]{1,0:T(8,128)(2,1)S(1)}, bf16[128,1024]{1,0:T(8,128)(2,1)S(1)}, u32[]{:S(2)}, u32[]{:S(2)}) collective-permute-start(bf16[128,1024]{1,0:T(8,128)(2,1)S(1)} %get-tuple-element.66), channel_id=1, source_target_pairs={{0,4},{4,8},{8,12},{1,5},{5,9},{9,13},{2,6},{6,10},{10,14},{3,7},{... | collective-permute-start | bytes 786440 | tf_op jit(solution)/shard_map/ppermute | solution.py:31
  272.4 8.6 %collective-permute-start.20 = (bf16[128,1152]{1,0:T(8,128)(2,1)S(1)}, bf16[128,1152]{1,0:T(8,128)(2,1)S(1)}, u32[]{:S(2)}, u32[]{:S(2)}) collective-permute-start(bf16[128,1152]{1,0:T(8,128)(2,1)S(1)} %get-tuple-element.61), channel_id=1, source_target_pairs={{4,0},{8,4},{12,8},{5,1},{9,5},{13,9},{6,2},{10,6},{14,10},{7,3},{... | collective-permute-start | bytes 884744 | tf_op jit(solution)/shard_map/ppermute | solution.py:31
  274.4 8.6 %collective-permute-start.17 = (bf16[128,1152]{1,0:T(8,128)(2,1)S(1)}, bf16[128,1152]{1,0:T(8,128)(2,1)S(1)}, u32[]{:S(2)}, u32[]{:S(2)}) collective-permute-start(bf16[128,1152]{1,0:T(8,128)(2,1)S(1)} %get-tuple-element.60), channel_id=1, source_target_pairs={{0,4},{4,8},{8,12},{1,5},{5,9},{9,13},{2,6},{6,10},{10,14},{3,7},{... | collective-permute-start | bytes 884744 | tf_op jit(solution)/shard_map/ppermute | solution.py:31
